TPU v7x, 512 devices: a whole 4x8x8 slice. The times are simulated.
512 devices in a mesh: wide: 64 (over z, x, core), narrow: 8 (over y).
Axes of the slice: x: 4, y: 8, z: 8, core: 2. Of those that a mesh axis runs over, the one named last changes fastest.
Arguments:
- charges: float32 [64, 1048576], P(None, ('wide', 'narrow')), may hold values from -6 to 6
- leaf_angle: float32 [64, 65536], P(None, ('wide', 'narrow')), may hold values from -3.140625 to 3.140625
- lagrange: float32 [48, 64], replicated, may hold values from -0.75 to 0.75
- level_angle: float32 [2, 48, 65536], P(None, None, ('wide', 'narrow')), may hold values from -3.140625 to 3.140625
- level_self: float32 [2, 96, 96], replicated, may hold values from -0.4375 to 0.4375
- level_peer: float32 [2, 96, 96], replicated, may hold values from -0.4375 to 0.4375
- switch_angle: float32 [48, 65536], P(None, ('wide', 'narrow')), may hold values from -3.140625 to 3.140625
- switch_matrix: float32 [96, 96], replicated, may hold values from -0.625 to 0.625
- out_angle: float32 [64, 65536], P(None, ('wide', 'narrow')), may hold values from -3.140625 to 3.140625
- evaluate: float32 [64, 48], replicated, may hold values from -0.875 to 0.875
Outputs:
- field: bfloat16 [64, 1048576], P(None, ('wide', 'narrow'))
All inputs are finite; a program needn't handle non-finite values.
Results may differ from a plain program's by a relative error of at most 0.0049.
Values may be sent and summed in bfloat16 or wider, within the bound.
No kernel may reach another device: no remote copies, remote signals or barrier semaphores. Data moves between devices by JAX's collectives and lax.ppermute only.
A program may use at most 64 MiB of HBM per device.

v0:
```python
import jax
import jax.numpy as jnp
from jax import lax
from jax.sharding import PartitionSpec as P


def from_partner(value, axis, apart):
    mask = 2**apart
    pairs = [(source, source ^ mask) for source in range(lax.axis_size(axis))]
    return lax.ppermute(value, axis, pairs)


def product(left, right):
    return jnp.dot(left, right, precision=lax.Precision.HIGHEST, preferred_element_type=jnp.float32)


def rotate(boxes_state, phase_angle, per_box):
    rank = phase_angle.shape[0]
    cos_part = jnp.repeat(jnp.cos(phase_angle), per_box, axis=1)
    sin_part = jnp.repeat(jnp.sin(phase_angle), per_box, axis=1)
    real_part = boxes_state[:rank]
    imag_part = boxes_state[rank:]
    return jnp.concatenate(
        [cos_part * real_part - sin_part * imag_part, sin_part * real_part + cos_part * imag_part],
        axis=0,
    )


def butterfly_level(boxes_state, self_matrix, peer_matrix, phase_angle, bit, per_box):
    sent_state = boxes_state.astype(jnp.bfloat16)
    received = from_partner(sent_state, "narrow", bit)
    combined = product(self_matrix, boxes_state) + product(
        peer_matrix, received.astype(jnp.float32)
    )
    return rotate(combined, phase_angle, per_box)


def leaf_weights(lagrange, point_charges, point_angle, per_box):
    cos_leaf = jnp.repeat(jnp.cos(point_angle), per_box, axis=1)
    sin_leaf = jnp.repeat(jnp.sin(point_angle), per_box, axis=1)
    return jnp.concatenate(
        [product(lagrange, cos_leaf * point_charges), product(lagrange, sin_leaf * point_charges)],
        axis=0,
    )


def body(
    charges,
    leaf_angle,
    lagrange,
    level_angle,
    level_self,
    level_peer,
    switch_angle,
    switch_matrix,
    out_angle,
    evaluate,
):
    per_box = charges.shape[1] // leaf_angle.shape[1]
    rank = lagrange.shape[0]
    last_bit = lax.axis_size("narrow").bit_length() - 2
    boxes_state = leaf_weights(lagrange, charges, leaf_angle, per_box)
    boxes_state = butterfly_level(
        boxes_state, level_self[0], level_peer[0], level_angle[0], 0, per_box
    )
    boxes_state = lax.all_to_all(boxes_state, "wide", split_axis=1, concat_axis=1, tiled=True)
    boxes_state = rotate(product(switch_matrix, boxes_state), switch_angle, per_box)
    boxes_state = butterfly_level(
        boxes_state, level_self[1], level_peer[1], level_angle[1], last_bit, per_box
    )
    real_part = product(evaluate, boxes_state[:rank])
    imag_part = product(evaluate, boxes_state[rank:])
    cos_out = jnp.repeat(jnp.cos(out_angle), per_box, axis=1)
    sin_out = jnp.repeat(jnp.sin(out_angle), per_box, axis=1)
    return (cos_out * real_part - sin_out * imag_part).astype(jnp.bfloat16)


def solution(mesh):
    return jax.shard_map(
        body,
        mesh=mesh,
        in_specs=(
            P(None, ("wide", "narrow")),
            P(None, ("wide", "narrow")),
            P(),
            P(None, None, ("wide", "narrow")),
            P(),
            P(),
            P(None, ("wide", "narrow")),
            P(),
            P(None, ("wide", "narrow")),
            P(),
        ),
        out_specs=P(None, ("wide", "narrow")),
        check_vma=False,
    )
```

profile of v0, /device:TPU:17, one launch (start us, length us, event | category | flops | bytes accessed | tf_op | source)
XLA Modules:
  0.0 94.2 jit_solution(16708297158461650053)
XLA Ops:
  0.0 0.9 fusion.31
  1.1 1.4 %copy.16 = f32[64,2048]{0,1:T(8,128)S(1)} copy(f32[64,2048]{1,0:T(8,128)} %param.10) | data formatting | bytes 1048576 | tf_op args[0]
  2.6 0.6 copy-done.9
  3.2 1.3 %convolution_bitcast_fusion.3 = f32[48,2048]{1,0:T(8,128)S(1)} fusion(f32[64,2048]{0,1:T(8,128)S(1)} %get-tuple-element.10, f32[48,64]{1,0:T(8,128)S(1)} %copy-done.9), kind=kOutput, calls=%fused_computation.11 | convolution fusion | flops 75497472 | bytes 929792 | tf_op jit(solution)/shard_map/dot_general | solution.py:14
  4.5 1.3 %convolution_bitcast_fusion.4 = f32[48,2048]{1,0:T(8,128)S(1)} fusion(f32[64,2048]{0,1:T(8,128)S(1)} %get-tuple-element.9, f32[48,64]{1,0:T(8,128)S(1)} %copy-done.9), kind=kOutput, calls=%fused_computation.12 | convolution fusion | flops 75497472 | bytes 929792 | tf_op jit(solution)/shard_map/dot_general | solution.py:14
  5.8 3.2 %collective-permute-start = (bf16[96,2048]{1,0:T(8,128)(2,1)S(1)}, bf16[96,2048]{1,0:T(8,128)(2,1)S(1)}, u32[]{:S(2)}, u32[]{:S(2)}) collective-permute-start(bf16[96,2048]{1,0:T(8,128)(2,1)S(1)} %fusion.8), channel_id=1, source_target_pairs={{0,1},{1,0},{2,3},{3,2},{4,5},{5,4},{6,7},{7,6},{8,9},{9,8},{10,11... | collective-permute-start | bytes 1179656 | tf_op jit(solution)/shard_map/ppermute | solution.py:10
  9.0 0.8 sine_bitcast_fusion.1
  10.0 0.3 copy.19
  10.5 0.3 copy.21
  10.8 0.6 copy-done.4
  11.4 0.8 fusion.9
  12.3 5.4 %collective-permute-done = bf16[96,2048]{1,0:T(8,128)(2,1)S(1)} collective-permute-done((bf16[96,2048]{1,0:T(8,128)(2,1)S(1)}, bf16[96,2048]{1,0:T(8,128)(2,1)S(1)}, u32[]{:S(2)}, u32[]{:S(2)}) %collective-permute-start) | collective-permute-done | bytes 393248 | tf_op jit(solution)/shard_map/ppermute | solution.py:10
  17.7 0.5 fusion.1
  18.3 1.3 %copy.24 = f32[96,2048]{0,1:T(8,128)} copy(f32[96,2048]{1,0:T(8,128)S(1)} %pad_maximum_fusion.1) | data formatting | bytes 1572864 | tf_op jit(solution)/shard_map/concatenate | solution.py:23
  19.7 15.0 %all-to-all-start = ((f32[96,64,32]{0,2,1:T(8,128)}), f32[96,64,32]{0,2,1:T(8,128)S(1)}, u32[]{:S(2)}, u32[]{:S(2)}) async-start(f32[96,64,32]{0,2,1:T(8,128)} %bitcast.15), calls=%async_computation | async-start | bytes 2097152 | tf_op jit(solution)/shard_map/all_to_all | solution.py:66
  35.0 0.3 copy.25
  35.5 1.1 %copy.27 = f32[48,2048]{1,0:T(8,128)} copy(f32[48,2048]{0,1:T(8,128)S(1)} %bitcast.70) | data formatting | bytes 786432 | tf_op jit(solution)/shard_map/reshape | solution.py:20
  36.8 0.3 copy.30
  37.1 0.4 copy-done.5
  37.7 0.3 copy.32
  38.0 24.7 %all-to-all-done = f32[96,64,32]{0,2,1:T(8,128)S(1)} async-done(((f32[96,64,32]{0,2,1:T(8,128)}), f32[96,64,32]{0,2,1:T(8,128)S(1)}, u32[]{:S(2)}, u32[]{:S(2)}) %all-to-all-start) | async-done | bytes 786464 | tf_op jit(solution)/shard_map/all_to_all | solution.py:66
  62.7 1.2 %convolution_bitcast_fusion = f32[96,2048]{1,0:T(8,128)S(1)} fusion(f32[96,2048]{0,1:T(8,128)S(1)} %bitcast.66, f32[96,96]{1,0:T(8,128)S(1)} %copy-done), kind=kOutput, calls=%fused_computation | convolution fusion | flops 226492416 | bytes 1609728 | tf_op jit(solution)/shard_map/dot_general | solution.py:14
  64.0 0.8 fusion.6
  64.8 5.8 %collective-permute-start.1 = (bf16[96,2048]{1,0:T(8,128)(2,1)}, bf16[96,2048]{1,0:T(8,128)(2,1)}, u32[]{:S(2)}, u32[]{:S(2)}) collective-permute-start(bf16[96,2048]{1,0:T(8,128)(2,1)} %fusion.6), channel_id=1, source_target_pairs={{0,4},{1,5},{2,6},{3,7},{4,0},{5,1},{6,2},{7,3},{8,12},{9,13},{10,... | collective-permute-start | bytes 1179656 | tf_op jit(solution)/shard_map/ppermute | solution.py:10
  71.0 0.3 copy.33
  71.5 1.1 %copy.37 = f32[64,2048]{1,0:T(8,128)} copy(f32[64,2048]{0,1:T(8,128)S(1)} %bitcast.74) | data formatting | bytes 1048576 | tf_op jit(solution)/shard_map/reshape | solution.py:74
  72.6 0.8 fusion.7
  73.5 16.9 %collective-permute-done.1 = bf16[96,2048]{1,0:T(8,128)(2,1)} collective-permute-done((bf16[96,2048]{1,0:T(8,128)(2,1)}, bf16[96,2048]{1,0:T(8,128)(2,1)}, u32[]{:S(2)}, u32[]{:S(2)}) %collective-permute-start.1) | collective-permute-done | bytes 393248 | tf_op jit(solution)/shard_map/ppermute | solution.py:10
  90.4 1.5 %fusion = f32[96,2048]{1,0:T(8,128)S(1)} fusion(f32[2048,96]{0,1:T(8,128)S(1)} %fusion.7, bf16[96,2048]{1,0:T(8,128)(2,1)} %collective-permute-done.1, f32[2,96,96]{2,1,0:T(8,128)S(1)} %copy-done.8), kind=kOutput, calls=%fused_computation.2 | convolution fusion | flops 226689024 | bytes 2015232 | tf_op jit(solution)/shard_map/dot_general | solution.py:14
  91.9 0.6 fusion.4
  92.5 0.4 copy-done.1
  92.9 1.3 %fusion.5 = bf16[64,2048]{1,0:T(8,128)(2,1)} fusion(f32[64,2048]{1,0:T(8,128)S(1)} %fusion.4, f32[64,2048]{1,0:T(8,128)S(1)} %copy-done.1, f32[64,48]{0,1:T(8,128)S(1)} %copy-done.3, f32[48,2048]{1,0:T(8,128)S(1)} %copy.30, f32[48,2048]{1,0:T(8,128)S(1)} %copy.32, f32[96,2048]{1,0:T(8,128)S(1)} %fusion), kind=kOutput, calls=%fused_computation.10 | convolution fusion | flops 76185600 | bytes 2895872 | tf_op jit(solution)/shard_map/dot_general | solution.py:14
  (47 shorter events, 2.2 us)
Async XLA Ops:
  0.0 62.7 %copy-start = (f32[96,96]{1,0:T(8,128)S(1)}, f32[96,96]{1,0:T(8,128)}, u32[]{:S(2)}) copy-start(f32[96,96]{1,0:T(8,128)} %param.17) | copy-start | bytes 110596
  2.5 0.7 copy-start.9
  5.8 3.3 %copy-start.10 = (f32[2,48,128]{2,1,0:T(8,128)S(1)}, f32[2,48,128]{2,1,0:T(8,128)}, u32[]{:S(2)}) copy-start(f32[2,48,128]{2,1,0:T(8,128)} %param.13) | copy-start | bytes 147460
  5.8 11.9 %collective-permute-start = (bf16[96,2048]{1,0:T(8,128)(2,1)S(1)}, bf16[96,2048]{1,0:T(8,128)(2,1)S(1)}, u32[]{:S(2)}, u32[]{:S(2)}) collective-permute-start(bf16[96,2048]{1,0:T(8,128)(2,1)S(1)} %fusion.8), channel_id=1, source_target_pairs={{0,1},{1,0},{2,3},{3,2},{4,5},{5,4},{6,7},{7,6},{8,9},{9,8},{10,11... | collective-permute-start | bytes 1179656 | tf_op jit(solution)/shard_map/ppermute | solution.py:10
  10.5 0.9 copy-start.4
  11.4 6.3 %copy-start.7 = (f32[2,96,96]{2,1,0:T(8,128)S(1)}, f32[2,96,96]{2,1,0:T(8,128)}, u32[]{:S(2)}) copy-start(f32[2,96,96]{2,1,0:T(8,128)} %param.15) | copy-start | bytes 221188
  19.7 15.0 %copy-start.12 = (f32[48,128]{1,0:T(8,128)S(1)}, f32[48,128]{1,0:T(8,128)}, u32[]{:S(2)}) copy-start(f32[48,128]{1,0:T(8,128)} %param.16) | copy-start | bytes 73732
  19.7 43.0 %all-to-all-start = ((f32[96,64,32]{0,2,1:T(8,128)}), f32[96,64,32]{0,2,1:T(8,128)S(1)}, u32[]{:S(2)}, u32[]{:S(2)}) async-start(f32[96,64,32]{0,2,1:T(8,128)} %bitcast.15), calls=%async_computation | async-start | bytes 2097152 | tf_op jit(solution)/shard_map/all_to_all | solution.py:66
  35.5 1.1 %copy-start.6 = (f32[48,128]{1,0:T(8,128)S(1)}, f32[48,128]{1,0:T(8,128)}, u32[]{:S(2)}) copy-start(f32[48,128]{1,0:T(8,128)} %get-tuple-element.14) | copy-start | bytes 73732
  36.7 0.7 copy-start.5
  62.7 1.2 %copy-start.2 = (f32[48,2048]{1,0:T(8,128)S(1)}, f32[48,2048]{1,0:T(8,128)}, u32[]{:S(2)}) copy-start(f32[48,2048]{1,0:T(8,128)} %copy.27) | copy-start | bytes 1179652
  64.0 6.7 %copy-start.11 = (f32[64,128]{1,0:T(8,128)S(1)}, f32[64,128]{1,0:T(8,128)}, u32[]{:S(2)}) copy-start(f32[64,128]{1,0:T(8,128)} %param.18) | copy-start | bytes 98308
  64.8 25.5 %collective-permute-start.1 = (bf16[96,2048]{1,0:T(8,128)(2,1)}, bf16[96,2048]{1,0:T(8,128)(2,1)}, u32[]{:S(2)}, u32[]{:S(2)}) collective-permute-start(bf16[96,2048]{1,0:T(8,128)(2,1)} %fusion.6), channel_id=1, source_target_pairs={{0,4},{1,5},{2,6},{3,7},{4,0},{5,1},{6,2},{7,3},{8,12},{9,13},{10,... | collective-permute-start | bytes 1179656 | tf_op jit(solution)/shard_map/ppermute | solution.py:10
  72.6 17.8 %copy-start.8 = (f32[2,96,96]{2,1,0:T(8,128)S(1)}, f32[2,96,96]{2,1,0:T(8,128)}, u32[]{:S(2)}) copy-start(f32[2,96,96]{2,1,0:T(8,128)} %param.15) | copy-start | bytes 221188
  73.5 18.4 %copy-start.3 = (f32[64,48]{0,1:T(8,128)S(1)}, f32[64,48]{0,1:T(8,128)}, u32[]{:S(2)}) copy-start(f32[64,48]{0,1:T(8,128)} %param.19) | copy-start | bytes 36868
  91.9 1.0 %copy-start.1 = (f32[64,2048]{1,0:T(8,128)S(1)}, f32[64,2048]{1,0:T(8,128)}, u32[]{:S(2)}) copy-start(f32[64,2048]{1,0:T(8,128)} %copy.37) | copy-start | bytes 1572868
where the time goes:
time: 94.9 us; the launch traced here: 94.2 us
  waiting for transfers between devices  47.1 us (50%)
  starting transfers between devices  24 us (25%)
  local copies, waits for them, and re-layouts  12.2 us (13%)
  matrix products  9.29 us (10%)
  other arithmetic  1.23 us (1%)
    all_to_all x1, waiting for transfers between devices, body(): lax.all_to_all(boxes_state, 'wide', split_axis=1, concat_axis=1, tiled=True)  24.7 us
    ppermute x2, waiting for transfers between devices, from_partner(): return lax.ppermute(value, axis, pairs)  22.4 us
    all_to_all x1, starting transfers between devices, body(): lax.all_to_all(boxes_state, 'wide', split_axis=1, concat_axis=1, tiled=True)  15 us
    dot_general x9, matrix products, product(): jnp.dot(left, right, precision=lax.Precision.HIGHEST, preferred_element_t...  9.29 us
    ppermute x2, starting transfers between devices, from_partner(): return lax.ppermute(value, axis, pairs)  9.03 us
    unnamed x27, local copies, waits for them, and re-layouts  3.41 us
  transfers between devices with their start and end apart: 3, of which 3 were waited for; matrix products, arithmetic and copies ran while one was open for 9% of the time, Pallas kernels for 0%

commit v1 on v0

--- a/solution.py
+++ b/solution.py
@@ -1,7 +1,19 @@
+import functools
 import jax
 import jax.numpy as jnp
 from jax import lax
 from jax.sharding import PartitionSpec as P
+
+
+def lay_bands(load, lane_axis):
+    local_now = lax.axis_size(lane_axis)
+    state_next = jnp.split(load, local_now, 1)
+    v1 = jnp.stack(state_next, 0)
+    item_now = lax.all_to_all(v1, lane_axis, 0, 0)
+    return jnp.concatenate(item_now, 1)
+
+
+see_row = functools.partial(lay_bands, lane_axis="wide")
 
 
 def from_partner(value, axis, apart):
@@ -63,7 +75,7 @@
     boxes_state = butterfly_level(
         boxes_state, level_self[0], level_peer[0], level_angle[0], 0, per_box
     )
-    boxes_state = lax.all_to_all(boxes_state, "wide", split_axis=1, concat_axis=1, tiled=True)
+    boxes_state = see_row(boxes_state)
     boxes_state = rotate(product(switch_matrix, boxes_state), switch_angle, per_box)
     boxes_state = butterfly_level(
         boxes_state, level_self[1], level_peer[1], level_angle[1], last_bit, per_box

time: 94.9 us -> 138 us (1.45)
  local copies, waits for them, and re-layouts: 12.2 us -> 54.1 us
    unnamed x27 -> x90, local copies, waits for them, and re-layouts: 3.41 us -> 41.3 us
    another operation x0 -> x65, local copies, waits for them, and re-layouts: none -> 5.38 us  [lay_bands(): v1 = jnp.stack(state_next, 0)]
  transfers between devices with their start and end apart: 3 -> 3, of which waited for: 3 -> 3; matrix products, arithmetic and copies ran while one was open for 9% -> 6% of each run, Pallas kernels for 0% -> 0%
where the time goes in v1:
time: 138 us; the launch traced here: 137 us
  local copies, waits for them, and re-layouts  54.1 us (39%)
  waiting for transfers between devices  47.1 us (34%)
  starting transfers between devices  24 us (17%)
  matrix products  9.28 us (7%)
  other arithmetic  2.22 us (2%)
    unnamed x90, local copies, waits for them, and re-layouts  41.3 us
    all_to_all x1, waiting for transfers between devices, lay_bands(): item_now = lax.all_to_all(v1, lane_axis, 0, 0)  24.7 us
    ppermute x2, waiting for transfers between devices, from_partner(): return lax.ppermute(value, axis, pairs)  22.3 us
    all_to_all x1, starting transfers between devices, lay_bands(): item_now = lax.all_to_all(v1, lane_axis, 0, 0)  15 us
    dot_general x9, matrix products, product(): jnp.dot(left, right, precision=lax.Precision.HIGHEST, preferred_element_t...  9.28 us
    ppermute x2, starting transfers between devices, from_partner(): return lax.ppermute(value, axis, pairs)  9.03 us
    another operation x65, local copies, waits for them, and re-layouts, lay_bands(): v1 = jnp.stack(state_next, 0)  5.38 us
  transfers between devices with their start and end apart: 3, of which 3 were waited for; matrix products, arithmetic and copies ran while one was open for 6% of the time, Pallas kernels for 0%

profile of v1, /device:TPU:17, one launch (start us, length us, event | category | flops | bytes accessed | tf_op | source)
XLA Modules:
  0.0 137.2 jit_solution(1930056417350603433)
XLA Ops:
  0.0 0.9 fusion.158
  1.1 1.4 %copy.43 = f32[64,2048]{0,1:T(8,128)S(1)} copy(f32[64,2048]{1,0:T(8,128)} %param.10) | data formatting | bytes 1048576 | tf_op args[0]
  3.2 1.3 convolution_bitcast_fusion.3
  4.5 1.3 convolution_bitcast_fusion.4
  5.8 3.2 %collective-permute-start = (bf16[96,2048]{1,0:T(8,128)(2,1)S(1)}, bf16[96,2048]{1,0:T(8,128)(2,1)S(1)}, u32[]{:S(2)}, u32[]{:S(2)}) collective-permute-start(bf16[96,2048]{1,0:T(8,128)(2,1)S(1)} %fusion.8), channel_id=1, source_target_pairs={{0,1},{1,0},{2,3},{3,2},{4,5},{5,4},{6,7},{7,6},{8,9},{9,8},{10,11... | collective-permute-start | bytes 1179656 | tf_op jit(solution)/shard_map/ppermute | solution.py:22
  9.0 0.8 sine_bitcast_fusion.1
  11.4 0.8 fusion.9
  12.3 5.4 %collective-permute-done = bf16[96,2048]{1,0:T(8,128)(2,1)S(1)} collective-permute-done((bf16[96,2048]{1,0:T(8,128)(2,1)S(1)}, bf16[96,2048]{1,0:T(8,128)(2,1)S(1)}, u32[]{:S(2)}, u32[]{:S(2)}) %collective-permute-start) | collective-permute-done | bytes 393248 | tf_op jit(solution)/shard_map/ppermute | solution.py:22
  19.4 0.6 constant_dynamic-update-slice_fusion.63
  24.8 0.6 constant_dynamic-update-slice_fusion.62
  26.0 0.6 constant_dynamic-update-slice_fusion.60
  31.4 0.6 constant_dynamic-update-slice_fusion.51
  42.2 0.6 constant_dynamic-update-slice_fusion.33
  42.9 0.6 constant_dynamic-update-slice_fusion.32
  46.5 0.6 constant_dynamic-update-slice_fusion.26
  47.7 0.6 constant_dynamic-update-slice_fusion.24
  50.7 0.6 constant_dynamic-update-slice_fusion.19
  52.5 0.6 constant_dynamic-update-slice_fusion.16
  60.3 0.6 constant_dynamic-update-slice_fusion.3
  62.1 0.6 constant_dynamic-update-slice_fusion
  62.7 15.0 %all-to-all-start = ((f32[64,96,32]{1,2,0:T(8,128)}), f32[64,96,32]{1,2,0:T(8,128)S(1)}, u32[]{:S(2)}, u32[]{:S(2)}) async-start(f32[64,96,32]{1,2,0:T(8,128)} %constant_dynamic-update-slice_fusion), calls=%async_computation | async-start | bytes 2097152 | tf_op jit(solution)/shard_map/all_to_all | solution.py:12
  78.5 1.1 copy.117
  81.0 24.7 %all-to-all-done = f32[64,96,32]{1,2,0:T(8,128)S(1)} async-done(((f32[64,96,32]{1,2,0:T(8,128)}), f32[64,96,32]{1,2,0:T(8,128)S(1)}, u32[]{:S(2)}, u32[]{:S(2)}) %all-to-all-start) | async-done | bytes 786464 | tf_op jit(solution)/shard_map/all_to_all | solution.py:12
  105.7 1.2 convolution_bitcast_fusion
  107.1 0.8 fusion.6
  107.9 5.8 %collective-permute-start.1 = (bf16[96,2048]{1,0:T(8,128)(2,1)}, bf16[96,2048]{1,0:T(8,128)(2,1)}, u32[]{:S(2)}, u32[]{:S(2)}) collective-permute-start(bf16[96,2048]{1,0:T(8,128)(2,1)} %fusion.6), channel_id=1, source_target_pairs={{0,4},{1,5},{2,6},{3,7},{4,0},{5,1},{6,2},{7,3},{8,12},{9,13},{10,... | collective-permute-start | bytes 1179656 | tf_op jit(solution)/shard_map/ppermute | solution.py:22
  114.5 1.1 copy.127
  115.7 0.8 fusion.7
  116.5 16.9 %collective-permute-done.1 = bf16[96,2048]{1,0:T(8,128)(2,1)} collective-permute-done((bf16[96,2048]{1,0:T(8,128)(2,1)}, bf16[96,2048]{1,0:T(8,128)(2,1)}, u32[]{:S(2)}, u32[]{:S(2)}) %collective-permute-start.1) | collective-permute-done | bytes 393248 | tf_op jit(solution)/shard_map/ppermute | solution.py:22
  133.4 1.4 %fusion = f32[96,2048]{1,0:T(8,128)S(1)} fusion(f32[2048,96]{0,1:T(8,128)S(1)} %fusion.7, bf16[96,2048]{1,0:T(8,128)(2,1)} %collective-permute-done.1, f32[2,96,96]{2,1,0:T(8,128)S(1)} %copy-done.8), kind=kOutput, calls=%fused_computation.128 | convolution fusion | flops 226689024 | bytes 2015232 | tf_op jit(solution)/shard_map/dot_general | solution.py:26
  134.9 0.6 fusion.4
  135.9 1.3 fusion.5
  (181 shorter events, 43.4 us)
Async XLA Ops:
  0.0 105.7 %copy-start = (f32[96,96]{1,0:T(8,128)S(1)}, f32[96,96]{1,0:T(8,128)}, u32[]{:S(2)}) copy-start(f32[96,96]{1,0:T(8,128)} %param.17) | copy-start | bytes 110596
  2.5 0.7 copy-start.9
  5.8 3.3 %copy-start.10 = (f32[2,48,128]{2,1,0:T(8,128)S(1)}, f32[2,48,128]{2,1,0:T(8,128)}, u32[]{:S(2)}) copy-start(f32[2,48,128]{2,1,0:T(8,128)} %param.13) | copy-start | bytes 147460
  5.8 11.9 %collective-permute-start = (bf16[96,2048]{1,0:T(8,128)(2,1)S(1)}, bf16[96,2048]{1,0:T(8,128)(2,1)S(1)}, u32[]{:S(2)}, u32[]{:S(2)}) collective-permute-start(bf16[96,2048]{1,0:T(8,128)(2,1)S(1)} %fusion.8), channel_id=1, source_target_pairs={{0,1},{1,0},{2,3},{3,2},{4,5},{5,4},{6,7},{7,6},{8,9},{9,8},{10,11... | collective-permute-start | bytes 1179656 | tf_op jit(solution)/shard_map/ppermute | solution.py:22
  10.5 0.9 copy-start.4
  11.4 6.3 %copy-start.7 = (f32[2,96,96]{2,1,0:T(8,128)S(1)}, f32[2,96,96]{2,1,0:T(8,128)}, u32[]{:S(2)}) copy-start(f32[2,96,96]{2,1,0:T(8,128)} %param.15) | copy-start | bytes 221188
  62.7 15.0 %copy-start.12 = (f32[48,128]{1,0:T(8,128)S(1)}, f32[48,128]{1,0:T(8,128)}, u32[]{:S(2)}) copy-start(f32[48,128]{1,0:T(8,128)} %param.16) | copy-start | bytes 73732
  62.7 43.0 %all-to-all-start = ((f32[64,96,32]{1,2,0:T(8,128)}), f32[64,96,32]{1,2,0:T(8,128)S(1)}, u32[]{:S(2)}, u32[]{:S(2)}) async-start(f32[64,96,32]{1,2,0:T(8,128)} %constant_dynamic-update-slice_fusion), calls=%async_computation | async-start | bytes 2097152 | tf_op jit(solution)/shard_map/all_to_all | solution.py:12
  78.5 1.1 copy-start.6
  79.7 0.7 copy-start.5
  105.7 1.2 copy-start.2
  107.0 6.6 %copy-start.11 = (f32[64,128]{1,0:T(8,128)S(1)}, f32[64,128]{1,0:T(8,128)}, u32[]{:S(2)}) copy-start(f32[64,128]{1,0:T(8,128)} %param.18) | copy-start | bytes 98308
  107.9 25.5 %collective-permute-start.1 = (bf16[96,2048]{1,0:T(8,128)(2,1)}, bf16[96,2048]{1,0:T(8,128)(2,1)}, u32[]{:S(2)}, u32[]{:S(2)}) collective-permute-start(bf16[96,2048]{1,0:T(8,128)(2,1)} %fusion.6), channel_id=1, source_target_pairs={{0,4},{1,5},{2,6},{3,7},{4,0},{5,1},{6,2},{7,3},{8,12},{9,13},{10,... | collective-permute-start | bytes 1179656 | tf_op jit(solution)/shard_map/ppermute | solution.py:22
  115.6 17.8 %copy-start.8 = (f32[2,96,96]{2,1,0:T(8,128)S(1)}, f32[2,96,96]{2,1,0:T(8,128)}, u32[]{:S(2)}) copy-start(f32[2,96,96]{2,1,0:T(8,128)} %param.15) | copy-start | bytes 221188
  116.5 18.4 %copy-start.3 = (f32[64,48]{0,1:T(8,128)S(1)}, f32[64,48]{0,1:T(8,128)}, u32[]{:S(2)}) copy-start(f32[64,48]{0,1:T(8,128)} %param.19) | copy-start | bytes 36868
  134.9 1.0 copy-start.1
